TPU v7x, 32 devices: a whole 2x2x4 slice. The times are simulated.
32 devices in a mesh: mem: 4 (over y, core), lat: 2 (over x), lon: 4 (over z).
Axes of the slice: x: 2, y: 2, z: 4, core: 2. Of those that a mesh axis runs over, the one named last changes fastest.
Arguments:
- perturbations: bfloat16 [8, 4, 768, 1536], P('mem', None, 'lat', 'lon'), may hold values from -2 to 2
- innovation: float32 [2, 8192], P('lat', 'lon'), may hold values from -4.2 to 4.2
- obs_weight: float32 [2, 8192], P('lat', 'lon'), may hold values from 0.5 to 6, as said below
- obs_cell: int32 [2, 8192], P('lat', 'lon'), may hold values from 0 to 147455
- obs_level: int32 [2, 8192], P('lat', 'lon'), may hold values from 0 to 3
- cutoff: int32 [4], replicated, may hold values from 16 to 127
Outputs:
- solution: float32 [8, 4, 768, 512], P('mem', None, ('lat', 'lon'))
- residual: float32 [8, 4, 768, 512], P('mem', None, ('lat', 'lon'))
Inputs may be any that keep to these rules, and one draw needn't show every extreme that they name: `obs_weight`: positive weights.
All inputs are finite; a program needn't handle non-finite values.
Results may differ from a plain program's by a relative error of at most 0.0008.
Values may be sent and summed in bfloat16 or wider, within the bound.
No kernel may reach another device: no remote copies, remote signals or barrier semaphores. Data moves between devices by JAX's collectives and lax.ppermute only.
A program may use at most 64 MiB of HBM per device.

v0:
```python
import jax
import jax.numpy as jnp
from jax import lax
from jax.sharding import PartitionSpec as P

NLON = 1536
KMAX = 256
ITERS = 2


def basis_table(transposed):
    factor = 2.0 * jnp.pi / NLON
    if transposed:
        columns = jnp.arange(NLON, dtype=jnp.int32)[None, :]
        cos_waves = jnp.arange(KMAX, dtype=jnp.int32)[:, None]
        axis_join = 0
    else:
        columns = jnp.arange(NLON, dtype=jnp.int32)[:, None]
        cos_waves = jnp.arange(KMAX, dtype=jnp.int32)[None, :]
        axis_join = 1
    cos_phase = (columns * cos_waves % NLON).astype(jnp.float32) * factor
    sin_phase = (columns * (cos_waves + 1) % NLON).astype(jnp.float32) * factor
    joined = jnp.concatenate([jnp.cos(cos_phase), jnp.sin(sin_phase)], axis=axis_join)
    return joined / jnp.sqrt(jnp.float32(KMAX))


def spectrum_of(cutoff):
    wavenumbers = jnp.concatenate(
        [jnp.arange(KMAX, dtype=jnp.float32), jnp.arange(1, KMAX + 1, dtype=jnp.float32)]
    )
    scaled = wavenumbers[None, :] / cutoff.astype(jnp.float32)[:, None]
    return 1.0 / (1.0 + scaled * scaled)


def member_total(partial_value):
    return lax.psum(partial_value, "mem")


def norm_total(residual):
    return lax.psum(jnp.sum(residual * residual), ("mem", "lat", "lon"))


def body(perturbations, innovation, obs_weight, obs_cell, obs_level, cutoff):
    members_here, levels, tile_rows, tile_cols = perturbations.shape
    line_rows = tile_rows // lax.axis_size("lon")
    basis_rows = basis_table(False)
    basis_cols = basis_table(True)
    spectrum = spectrum_of(cutoff)
    located = (obs_level * (tile_rows * tile_cols) + obs_cell).reshape(-1)
    weights = obs_weight.reshape(-1)

    def gridded_of(weighted):
        field = jnp.zeros((levels * tile_rows * tile_cols,), jnp.float32).at[located].add(weighted)
        return field.reshape(levels, tile_rows, tile_cols)

    def analyse(products):
        summed = jnp.dot(
            products.reshape(-1, NLON),
            basis_rows,
            precision=lax.Precision.HIGHEST,
            preferred_element_type=jnp.float32,
        )
        return (
            summed.reshape(members_here, levels, line_rows, 2 * KMAX) * spectrum[None, :, None, :]
        )

    line_pert = lax.all_to_all(perturbations, "lon", split_axis=2, concat_axis=3, tiled=True)

    def adjoint_part(gridded):
        grid_lines = lax.all_to_all(gridded, "lon", split_axis=1, concat_axis=2, tiled=True)
        products = line_pert.astype(jnp.float32) * grid_lines[None]
        return analyse(products)

    right_side = adjoint_part(gridded_of(weights * innovation.reshape(-1)))
    solution = jnp.zeros_like(right_side)
    residual = right_side
    direction = right_side
    norm_now = norm_total(residual)
    for iteration in range(ITERS):
        coeffs = direction * spectrum[None, :, None, :]
        synthesized = jnp.dot(
            coeffs.reshape(-1, 2 * KMAX),
            basis_cols,
            precision=lax.Precision.HIGHEST,
            preferred_element_type=jnp.float32,
        )
        forward_synthesized = synthesized.reshape(members_here, levels, line_rows, NLON)
        partial_value = jnp.sum(line_pert.astype(jnp.float32) * forward_synthesized, axis=0)
        on_tiles = lax.all_to_all(partial_value, "lon", split_axis=2, concat_axis=1, tiled=True)
        increment = member_total(on_tiles)
        sampled = increment.reshape(-1)[located]
        image = direction + adjoint_part(gridded_of(weights * sampled))
        curvature = lax.psum(jnp.sum(direction * image), ("mem", "lat", "lon"))
        step_size = norm_now / curvature
        solution = solution + step_size * direction
        residual = residual - step_size * image
        if iteration + 1 < ITERS:
            norm_next = norm_total(residual)
            direction = residual + norm_next / norm_now * direction
            norm_now = norm_next
    return (solution, residual)


def solution(mesh):
    placed = (
        P("mem", None, "lat", "lon"),
        P("lat", "lon"),
        P("lat", "lon"),
        P("lat", "lon"),
        P("lat", "lon"),
        P(),
    )
    return jax.shard_map(
        body,
        mesh=mesh,
        in_specs=placed,
        out_specs=(P("mem", None, ("lat", "lon"), None), P("mem", None, ("lat", "lon"), None)),
        check_vma=False,
    )
```

profile of v0, /device:TPU:0, one launch (start us, length us, event | category | flops | bytes accessed | tf_op | source)
XLA Modules:
  0.0 842.8 jit_solution(17484831876931123835)
XLA Ops:
  8.6 12.8 %scatter_custom_fusion = f32[589824]{0:T(1024)} fusion(s32[2048]{0:T(1024)S(1)} %bitcast.74, f32[2048]{0:T(1024)S(1)} %mul.200, f32[]{:T(128)} %constant.20.clone.1), kind=kCustom, calls=%fused_computation.75 | custom fusion | flops 2048 | bytes 2359300 | tf_op jit(solution)/shard_map/scatter-add | solution.py:53
  21.4 3.4 reshape.134
  24.8 4.6 copy.45
  29.4 6.3 all-to-all-start.1
  35.7 4.9 copy.43
  40.6 49.0 %all-to-all-done.1 = f32[4,384,384]{2,0,1:T(4,128)} async-done(((f32[4,384,384]{2,0,1:T(4,128)}), f32[4,384,384]{2,0,1:T(4,128)}, u32[]{:S(2)}, u32[]{:S(2)}) %all-to-all-start.1) | async-done | bytes 2359328 | tf_op jit(solution)/shard_map/all_to_all | solution.py:70
  89.6 4.5 all-to-all-start
  94.5 5.9 fusion.18
  100.4 8.1 fusion.24
  108.5 6.8 fusion.21
  115.3 7.0 fusion.27
  122.3 1.8 copy.46
  124.2 1.8 copy.66
  125.9 21.6 %all-to-all-done = bf16[2,4,384,384]{3,1,0,2:T(4,128)(2,1)} async-done(((bf16[2,4,384,384]{3,1,0,2:T(4,128)(2,1)}), bf16[2,4,384,384]{3,1,0,2:T(4,128)(2,1)}, u32[]{:S(2)}, u32[]{:S(2)}) %all-to-all-start) | async-done | bytes 2359328 | tf_op jit(solution)/shard_map/all_to_all | solution.py:67
  147.6 5.7 copy.70
  153.3 6.4 reshape.141
  159.6 10.9 %fusion.47 = f32[2,4,96,512]{3,2,1,0:T(8,128)S(1)} fusion(f32[1536,256]{1,0:T(8,128)} %fusion.21, f32[1536,256]{1,0:T(8,128)S(1)} %fusion.18, f32[2,4,96,1536]{3,2,1,0:T(8,128)} %reshape.141, f32[4,96,1536]{2,1,0:T(8,128)} %bitcast.63, f32[4,512]{1,0:T(4,128)S(1)} %fusion.65), kind=kOutput, calls=%fused_computation.70 | convolution fusion | flops 7250903040 | bytes 11804672 | tf_op jit(solution)/shard_map/dot_general | solution.py:57
  170.6 10.3 %multiply_reduce_fusion.1 = f32[4,96,1536]{2,1,0:T(8,128)} fusion(f32[2,4,96,1536]{3,2,1,0:T(8,128)S(1)} %copy-done, f32[256,1536]{1,0:T(8,128)S(1)} %copy-done.10, f32[256,1536]{1,0:T(8,128)S(1)} %copy-done.8, f32[2,4,96,512]{3,2,1,0:T(8,128)S(1)} %fusion.47, f32[4,512]{1,0:T(4,128)S(1)} %fusion.65), kind=kOutput, calls=%fused_computation.11 | convolution fusion | flops 7251492864 | bytes 11804672 | tf_op jit(solution)/shard_map/dot_general | solution.py:81
  180.9 4.5 copy.48
  185.4 75.5 %all_to_all.90 = f32[4,96,1536]{1,0,2:T(4,128)} all-to-all(f32[4,96,1536]{1,0,2:T(4,128)} %copy.48), channel_id=1, replica_groups=mesh['mem'=4,'lat'=2,'lon'=4] {'lon'}, dimensions={2} | all-to-all | bytes 4718592 | tf_op jit(solution)/shard_map/all_to_all | solution.py:89
  261.0 4.7 copy.50
  265.6 3.2 reshape.135
  269.0 54.8 %all-reduce.4.cloned.1.call-done = f32[589824]{0:T(1024)} async-done(((f32[589824]{0:T(1024)}), f32[589824]{0:T(1024)}) %all-reduce.4.cloned.1.call-update) | async-done | bytes 2359312 | tf_op jit(solution)/shard_map/psum | solution.py:36
  323.8 24.5 %gather_fusion = f32[2048]{0:T(1024)S(1)} fusion(f32[589824]{0:T(1024)} %all-reduce.4.cloned.1.call-done, s32[2048]{0:T(1024)S(1)} %broadcast_clamp_fusion), kind=kCustom, calls=%fused_computation | custom fusion | bytes 24576 | tf_op jit(solution)/shard_map/gather | solution.py:91
  348.3 12.8 %scatter_custom_fusion.1 = f32[589824]{0:T(1024)} fusion(s32[2048]{0:T(1024)S(1)} %bitcast.76, f32[2048]{0:T(1024)S(1)} %mul.226, f32[]{:T(128)} %constant.20.clone.1), kind=kCustom, calls=%fused_computation.73 | custom fusion | flops 2048 | bytes 2359300 | tf_op jit(solution)/shard_map/scatter-add | solution.py:53
  361.1 3.4 reshape.136
  364.5 3.2 copy.51
  367.7 58.7 %all_to_all.91 = f32[4,384,384]{2,0,1:T(4,128)S(1)} all-to-all(f32[4,384,384]{2,0,1:T(4,128)S(1)} %copy.51), channel_id=1, replica_groups=mesh['mem'=4,'lat'=2,'lon'=4] {'lon'}, dimensions={1} | all-to-all | bytes 4718592 | tf_op jit(solution)/shard_map/all_to_all | solution.py:70
  428.5 8.6 %multiply_reduce_fusion.4 = (f32[]{:T(128)}, f32[]{:T(128)}, f32[2,4,96,512]{3,2,1,0:T(8,128)S(1)}) fusion(f32[2,4,96,512]{3,2,1,0:T(8,128)S(1)} %fusion.47, f32[4,512]{1,0:T(4,128)S(1)} %fusion.65, f32[1536,256]{1,0:T(8,128)S(1)} %copy-done.4, f32[1536,256]{1,0:T(8,128)S(1)} %copy-done.2, f32[2,4,96,1536]{3,2,1,0:T(8,128)S(1)} %bitcast.59, ...), kind=kOutput, calls=%fused_computation.45 | convolution fusion | flops 7252869120 | bytes 13377544 | tf_op jit(solution)/shard_map/dot_general | solution.py:57
  437.1 38.3 %all-reduce = (f32[]{:T(128)}, f32[]{:T(128)}) all-reduce(f32[]{:T(128)} %get-tuple-element.3, f32[]{:T(128)} %get-tuple-element.2), channel_id=1, replica_groups=mesh['mem'=4,'lat'=2,'lon'=4] {'mem','lat','lon'}, use_global_device_ids=true, to_apply=%region_2.3 | all-reduce | flops 2 | bytes 16 | tf_op jit(solution)/shard_map/psum | solution.py:40
  476.8 1.1 multiply_reduce_fusion.3
  477.9 41.6 %psum.45 = f32[]{:T(128)} all-reduce(f32[]{:T(128)} %multiply_reduce_fusion.3), channel_id=1, replica_groups=mesh['mem'=4,'lat'=2,'lon'=4] {'mem','lat','lon'}, use_global_device_ids=true, to_apply=%region_9.10 | all-reduce | flops 1 | bytes 8 | tf_op jit(solution)/shard_map/psum | solution.py:40
  521.2 1.2 copy-done.6
  522.4 0.8 copy-done.11
  523.2 11.4 %multiply_reduce_fusion = f32[4,96,1536]{2,1,0:T(8,128)} fusion(f32[2,4,96,1536]{3,2,1,0:T(8,128)} %reshape.141, f32[256,1536]{1,0:T(8,128)S(1)} %copy-done.11, f32[256,1536]{1,0:T(8,128)S(1)} %copy-done.9, f32[2,4,96,512]{3,2,1,0:T(8,128)S(1)} %multiply_add_fusion.2, f32[4,512]{1,0:T(4,128)S(1)} %fusion.65), kind=kOutput, calls=%fused_computation.8 | convolution fusion | flops 7251492864 | bytes 11804672 | tf_op jit(solution)/shard_map/dot_general | solution.py:81
  534.6 4.5 copy.54
  539.1 75.7 %all_to_all.92 = f32[4,96,1536]{1,0,2:T(4,128)} all-to-all(f32[4,96,1536]{1,0,2:T(4,128)} %copy.54), channel_id=1, replica_groups=mesh['mem'=4,'lat'=2,'lon'=4] {'lon'}, dimensions={2} | all-to-all | bytes 4718592 | tf_op jit(solution)/shard_map/all_to_all | solution.py:89
  614.8 4.6 copy.56
  619.4 3.2 reshape.137
  622.7 54.8 %all-reduce.6.cloned.1.call-done = f32[589824]{0:T(1024)} async-done(((f32[589824]{0:T(1024)}), f32[589824]{0:T(1024)}) %all-reduce.6.cloned.1.call-update) | async-done | bytes 2359312 | tf_op jit(solution)/shard_map/psum | solution.py:36
  677.4 24.5 %gather_fusion.1 = f32[2048]{0:T(1024)S(1)} fusion(f32[589824]{0:T(1024)} %all-reduce.6.cloned.1.call-done, s32[2048]{0:T(1024)S(1)} %broadcast_clamp_fusion), kind=kCustom, calls=%fused_computation.1 | custom fusion | bytes 24576 | tf_op jit(solution)/shard_map/gather | solution.py:91
  701.9 12.8 %scatter_custom_fusion.2 = f32[589824]{0:T(1024)} fusion(s32[2048]{0:T(1024)S(1)} %bitcast.77, f32[2048]{0:T(1024)S(1)} %mul.240, f32[]{:T(128)} %constant.20.clone.1), kind=kCustom, calls=%fused_computation.71 | custom fusion | flops 2048 | bytes 2359300 | tf_op jit(solution)/shard_map/scatter-add | solution.py:53
  714.7 3.4 reshape.138
  718.1 3.2 copy.57
  721.3 58.4 %all_to_all.93 = f32[4,384,384]{2,0,1:T(4,128)S(1)} all-to-all(f32[4,384,384]{2,0,1:T(4,128)S(1)} %copy.57), channel_id=1, replica_groups=mesh['mem'=4,'lat'=2,'lon'=4] {'lon'}, dimensions={1} | all-to-all | bytes 4718592 | tf_op jit(solution)/shard_map/all_to_all | solution.py:70
  782.3 9.5 %multiply_reduce_fusion.2 = (f32[]{:T(128)}, f32[2,4,96,512]{3,2,1,0:T(8,128)}) fusion(f32[2,4,96,512]{3,2,1,0:T(8,128)S(1)} %copy-done.7, f32[4,512]{1,0:T(4,128)S(1)} %fusion.65, f32[1536,256]{1,0:T(8,128)S(1)} %copy-done.5, f32[1536,256]{1,0:T(8,128)S(1)} %copy-done.3, f32[2,4,96,1536]{3,2,1,0:T(8,128)S(1)} %bitcast.61, f32[4,96,1536]{2,1,0:T(8,128)S(1)} %bitcast.64), kind=kOutput, calls=%fused_computation.39 | convolution fusion | flops 7252082688 | bytes 13377540 | tf_op jit(solution)/shard_map/dot_general | solution.py:57
  791.8 38.3 %psum.47 = f32[]{:T(128)} all-reduce(f32[]{:T(128)} %get-tuple-element.9), channel_id=1, replica_groups=mesh['mem'=4,'lat'=2,'lon'=4] {'mem','lat','lon'}, use_global_device_ids=true, to_apply=%region_14.15 | all-reduce | flops 1 | bytes 8 | tf_op jit(solution)/shard_map/psum | solution.py:93
  831.4 4.3 multiply_subtract_fusion
  (56 shorter events, 6.8 us)
Async XLA Ops:
  29.4 60.3 %all-to-all-start.1 = ((f32[4,384,384]{2,0,1:T(4,128)}), f32[4,384,384]{2,0,1:T(4,128)}, u32[]{:S(2)}, u32[]{:S(2)}) async-start(f32[4,384,384]{2,0,1:T(4,128)} %copy.45), calls=%async_computation.1 | async-start | bytes 4718592 | tf_op jit(solution)/shard_map/all_to_all | solution.py:70
  40.6 53.8 %copy-start.13 = (s32[4]{0:T(128)S(1)}, s32[4]{0:T(128)}, u32[]{:S(2)}) copy-start(s32[4]{0:T(128)} %param.11) | copy-start | bytes 52
  89.6 57.9 %all-to-all-start = ((bf16[2,4,384,384]{3,1,0,2:T(4,128)(2,1)}), bf16[2,4,384,384]{3,1,0,2:T(4,128)(2,1)}, u32[]{:S(2)}, u32[]{:S(2)}) async-start(bf16[2,4,384,384]{3,1,0,2:T(4,128)(2,1)} %copy.43), calls=%async_computation | async-start | bytes 4718592 | tf_op jit(solution)/shard_map/all_to_all | solution.py:67
  94.1 229.7 %all-reduce.4.cloned.1.call-start = ((), (), s32[]{:S(2)}) async-start(), calls=%async_computation.6 | async-start | bytes 4718592 | tf_op jit(solution)/shard_map/psum | solution.py:36
  100.4 59.2 %copy-start.1 = (f32[1536,256]{1,0:T(8,128)}, f32[1536,256]{1,0:T(8,128)S(1)}, u32[]{:S(2)}) copy-start(f32[1536,256]{1,0:T(8,128)S(1)} %fusion.18) | copy-start | bytes 4718596
  159.6 10.9 %copy-start = (f32[2,4,96,1536]{3,2,1,0:T(8,128)S(1)}, f32[2,4,96,1536]{3,2,1,0:T(8,128)}, u32[]{:S(2)}) copy-start(f32[2,4,96,1536]{3,2,1,0:T(8,128)} %reshape.141) | copy-start | bytes 14155780
  159.6 10.9 %copy-start.8 = (f32[256,1536]{1,0:T(8,128)S(1)}, f32[256,1536]{1,0:T(8,128)}, u32[]{:S(2)}) copy-start(f32[256,1536]{1,0:T(8,128)} %fusion.24) | copy-start | bytes 4718596
  159.6 11.0 %copy-start.10 = (f32[256,1536]{1,0:T(8,128)S(1)}, f32[256,1536]{1,0:T(8,128)}, u32[]{:S(2)}) copy-start(f32[256,1536]{1,0:T(8,128)} %fusion.27) | copy-start | bytes 4718596
  268.9 408.5 %all-reduce.6.cloned.1.call-start = ((), (), s32[]{:S(2)}) async-start(), calls=%async_computation.7 | async-start | bytes 4718592 | tf_op jit(solution)/shard_map/psum | solution.py:36
  268.9 79.3 %copy-start.12 = (f32[1,2048]{1,0:T(1,128)S(1)}, f32[1,2048]{1,0:T(1,128)}, u32[]{:S(2)}) copy-start(f32[1,2048]{1,0:T(1,128)} %param.8) | copy-start | bytes 24580
  367.7 59.2 %slice-start = ((s8[4718592]{0:T(1024)(128)(4,1)}), s8[4194304]{0:T(1024)(128)(4,1)S(1)}, s32[]{:S(2)}) async-start(s8[4718592]{0:T(1024)(128)(4,1)} %bitcast.58), calls=%async_computation.8 | async-start | bytes 8388608
  426.4 1.0 slice-start.1
  426.6 1.4 copy-start.2
  426.6 1.9 copy-start.4
  520.8 1.6 copy-start.9
  520.8 2.4 copy-start.11
  521.2 1.2 copy-start.6
  721.3 59.0 %slice-start.2 = ((s8[4718592]{0:T(1024)(128)(4,1)}), s8[4194304]{0:T(1024)(128)(4,1)S(1)}, s32[]{:S(2)}) async-start(s8[4718592]{0:T(1024)(128)(4,1)} %bitcast.60), calls=%async_computation.10 | async-start | bytes 8388608
  779.7 1.0 slice-start.3
  779.9 1.4 copy-start.3
  779.9 1.9 copy-start.5
  779.9 2.4 copy-start.7
Sparse Core Ops, SparseCore 0:
  269.0 54.7 all-reduce.3
  622.8 54.5 all-reduce.5
where the time goes:
time: 851 us; the launch traced here: 843 us
  blocking collectives  387 us (45%)
  waiting for transfers between devices  180 us (21%)
  local copies, waits for them, and re-layouts  122 us (14%)
  other arithmetic  73.6 us (9%)
  matrix products  50.7 us (6%)
  between operations  18.6 us (2%)
  starting transfers between devices  11.1 us (1%)
    all_to_all x2, blocking collectives, body(): lax.all_to_all(partial_value, 'lon', split_axis=2, concat_axis=1, tiled=T...  151 us
    all_to_all x2, blocking collectives, adjoint_part(): lax.all_to_all(gridded, 'lon', split_axis=1, concat_axis=2, tiled=True)  117 us
    psum x2, waiting for transfers between devices, member_total(): return lax.psum(partial_value, 'mem')  110 us
    psum x2, blocking collectives, norm_total(): return lax.psum(jnp.sum(residual * residual), ('mem', 'lat', 'lon'))  79.9 us
    all_to_all x1, waiting for transfers between devices, adjoint_part(): lax.all_to_all(gridded, 'lon', split_axis=1, concat_axis=2, tiled=True)  49 us
    gather x2, local copies, waits for them, and re-layouts, body(): sampled = increment.reshape(-1)[located]  49 us
    scatter-add x3, other arithmetic, gridded_of(): jnp.zeros((levels * tile_rows * tile_cols,), jnp.float32).at[located]  38.4 us
    psum x1, blocking collectives, body(): curvature = lax.psum(jnp.sum(direction * image), ('mem', 'lat', 'lon'))  38.3 us
  transfers between devices with their start and end apart: 4, of which 4 were waited for; matrix products, arithmetic and copies ran while one was open for 4% of the time, Pallas kernels for 0%

commit v1 on v0

--- a/solution.py
+++ b/solution.py
@@ -86,7 +86,10 @@
         )
         forward_synthesized = synthesized.reshape(members_here, levels, line_rows, NLON)
         partial_value = jnp.sum(line_pert.astype(jnp.float32) * forward_synthesized, axis=0)
-        on_tiles = lax.all_to_all(partial_value, "lon", split_axis=2, concat_axis=1, tiled=True)
+        size = lax.axis_size("lon")
+        blocks = jnp.stack(jnp.split(partial_value, size, axis=2), axis=0)
+        blocks = lax.all_to_all(blocks, "lon", split_axis=0, concat_axis=0)
+        on_tiles = jnp.concatenate(blocks, axis=1)
         increment = member_total(on_tiles)
         sampled = increment.reshape(-1)[located]
         image = direction + adjoint_part(gridded_of(weights * sampled))

time: 851 us -> 793 us (0.932)
  blocking collectives: 387 us -> 347 us
  local copies, waits for them, and re-layouts: 122 us -> 107 us
    all_to_all x2, blocking collectives: 151 us -> 112 us  [body(): blocks = lax.all_to_all(blocks, 'lon', split_axis=0, concat_axis=0)]
    all_to_all x2 -> x0, local copies, waits for them, and re-layouts: 9.27 us -> none  [body(): lax.all_to_all(partial_value, 'lon', split_axis=2, concat_axis=1, tiled=T...]
    reduce_sum x2 -> x0, local copies, waits for them, and re-layouts: 9 us -> none  [body(): jnp.sum(line_pert.astype(jnp.float32) * forward_synthesized, axis=0)]
  transfers between devices with their start and end apart: 4 -> 4, of which waited for: 4 -> 4; matrix products, arithmetic and copies ran while one was open for 4% -> 5% of each run, Pallas kernels for 0% -> 0%
where the time goes in v1:
time: 793 us; the launch traced here: 786 us
  blocking collectives  347 us (44%)
  waiting for transfers between devices  180 us (23%)
  local copies, waits for them, and re-layouts  107 us (13%)
  other arithmetic  73.9 us (9%)
  matrix products  48.3 us (6%)
  between operations  18.2 us (2%)
  starting transfers between devices  11.1 us (1%)
    all_to_all x2, blocking collectives, adjoint_part(): lax.all_to_all(gridded, 'lon', split_axis=1, concat_axis=2, tiled=True)  117 us
    all_to_all x2, blocking collectives, body(): blocks = lax.all_to_all(blocks, 'lon', split_axis=0, concat_axis=0)  112 us
    psum x2, waiting for transfers between devices, member_total(): return lax.psum(partial_value, 'mem')  110 us
    psum x2, blocking collectives, norm_total(): return lax.psum(jnp.sum(residual * residual), ('mem', 'lat', 'lon'))  79.8 us
    all_to_all x1, waiting for transfers between devices, adjoint_part(): lax.all_to_all(gridded, 'lon', split_axis=1, concat_axis=2, tiled=True)  49 us
    gather x2, local copies, waits for them, and re-layouts, body(): sampled = increment.reshape(-1)[located]  49 us
    scatter-add x3, other arithmetic, gridded_of(): jnp.zeros((levels * tile_rows * tile_cols,), jnp.float32).at[located]  38.4 us
    psum x1, blocking collectives, body(): curvature = lax.psum(jnp.sum(direction * image), ('mem', 'lat', 'lon'))  38.3 us
  transfers between devices with their start and end apart: 4, of which 4 were waited for; matrix products, arithmetic and copies ran while one was open for 5% of the time, Pallas kernels for 0%

profile of v1, /device:TPU:0, one launch (start us, length us, event | category | flops | bytes accessed | tf_op | source)
XLA Modules:
  0.0 785.6 jit_solution(11554780191326104)
XLA Ops:
  7.2 0.7 mul.200
  7.9 0.7 compare_select_fusion
  8.6 12.8 %scatter_custom_fusion = f32[589824]{0:T(1024)} fusion(s32[2048]{0:T(1024)S(1)} %bitcast.84, f32[2048]{0:T(1024)S(1)} %mul.200, f32[]{:T(128)} %constant.20.clone.1), kind=kCustom, calls=%fused_computation.77 | custom fusion | flops 2048 | bytes 2359300 | tf_op jit(solution)/shard_map/scatter-add | solution.py:53
  21.4 3.4 reshape.146
  24.8 4.6 copy.38
  29.4 6.3 all-to-all-start.1
  35.7 4.9 copy.36
  40.6 49.0 %all-to-all-done.1 = f32[4,384,384]{2,0,1:T(4,128)} async-done(((f32[4,384,384]{2,0,1:T(4,128)}), f32[4,384,384]{2,0,1:T(4,128)}, u32[]{:S(2)}, u32[]{:S(2)}) %all-to-all-start.1) | async-done | bytes 2359328 | tf_op jit(solution)/shard_map/all_to_all | solution.py:70
  89.6 4.5 all-to-all-start
  94.5 5.9 fusion.18
  100.4 8.1 %fusion.24 = f32[256,1536]{1,0:T(8,128)} fusion(), kind=kLoop, calls=%fused_computation.35 | loop fusion | flops 3538944 | bytes 1572864 | tf_op jit(solution)/shard_map/cos | solution.py:23
  108.5 6.8 fusion.21
  115.3 7.0 fusion.27
  122.4 1.8 copy.39
  124.2 1.7 copy.51
  125.9 21.7 %all-to-all-done = bf16[2,4,384,384]{3,1,0,2:T(4,128)(2,1)} async-done(((bf16[2,4,384,384]{3,1,0,2:T(4,128)(2,1)}), bf16[2,4,384,384]{3,1,0,2:T(4,128)(2,1)}, u32[]{:S(2)}, u32[]{:S(2)}) %all-to-all-start) | async-done | bytes 2359328 | tf_op jit(solution)/shard_map/all_to_all | solution.py:67
  147.6 5.7 copy.55
  153.2 6.4 reshape.157
  159.6 10.9 %fusion.47 = f32[2,4,96,512]{3,2,1,0:T(8,128)S(1)} fusion(f32[1536,256]{1,0:T(8,128)} %fusion.21, f32[1536,256]{1,0:T(8,128)S(1)} %fusion.18, f32[2,4,96,1536]{3,2,1,0:T(8,128)} %reshape.157, f32[4,96,1536]{2,1,0:T(8,128)} %bitcast.73, f32[4,512]{1,0:T(4,128)S(1)} %fusion.65), kind=kOutput, calls=%fused_computation.72 | convolution fusion | flops 7250903040 | bytes 11804672 | tf_op jit(solution)/shard_map/dot_general | solution.py:57
  170.6 8.8 %multiply_reduce_fusion.1 = f32[4,96,1536]{2,1,0:T(8,128)S(1)} fusion(f32[2,4,96,1536]{3,2,1,0:T(8,128)S(1)} %copy-done, f32[256,1536]{1,0:T(8,128)S(1)} %copy-done.10, f32[256,1536]{1,0:T(8,128)S(1)} %copy-done.8, f32[2,4,96,512]{3,2,1,0:T(8,128)S(1)} %fusion.47, f32[4,512]{1,0:T(4,128)S(1)} %fusion.65), kind=kOutput, calls=%fused_computation.11 | convolution fusion | flops 7251492864 | bytes 11804672 | tf_op jit(solution)/shard_map/dot_general | solution.py:81
  179.8 55.9 %all_to_all.64 = f32[4,4,96,384]{3,2,1,0:T(8,128)S(1)} all-to-all(f32[4,4,96,384]{3,2,1,0:T(8,128)S(1)} %pad_maximum_fusion), channel_id=1, replica_groups=mesh['mem'=4,'lat'=2,'lon'=4] {'lon'}, dimensions={0} | all-to-all | bytes 4718592 | tf_op jit(solution)/shard_map/all_to_all | solution.py:91
  235.7 1.6 copy.41
  237.3 3.2 reshape.149
  240.6 54.8 %all-reduce.4.cloned.1.call-done = f32[589824]{0:T(1024)} async-done(((f32[589824]{0:T(1024)}), f32[589824]{0:T(1024)}) %all-reduce.4.cloned.1.call-update) | async-done | bytes 2359312 | tf_op jit(solution)/shard_map/psum | solution.py:36
  295.5 24.5 %gather_fusion = f32[2048]{0:T(1024)S(1)} fusion(f32[589824]{0:T(1024)} %all-reduce.4.cloned.1.call-done, s32[2048]{0:T(1024)S(1)} %broadcast_clamp_fusion), kind=kCustom, calls=%fused_computation | custom fusion | bytes 24576 | tf_op jit(solution)/shard_map/gather | solution.py:94
  320.0 12.8 %scatter_custom_fusion.1 = f32[589824]{0:T(1024)} fusion(s32[2048]{0:T(1024)S(1)} %bitcast.86, f32[2048]{0:T(1024)S(1)} %mul.226, f32[]{:T(128)} %constant.20.clone.1), kind=kCustom, calls=%fused_computation.75 | custom fusion | flops 2048 | bytes 2359300 | tf_op jit(solution)/shard_map/scatter-add | solution.py:53
  332.8 3.4 reshape.150
  336.2 3.2 copy.42
  339.4 58.7 %all_to_all.65 = f32[4,384,384]{2,0,1:T(4,128)S(1)} all-to-all(f32[4,384,384]{2,0,1:T(4,128)S(1)} %copy.42), channel_id=1, replica_groups=mesh['mem'=4,'lat'=2,'lon'=4] {'lon'}, dimensions={1} | all-to-all | bytes 4718592 | tf_op jit(solution)/shard_map/all_to_all | solution.py:70
  400.2 8.6 %multiply_reduce_fusion.4 = (f32[]{:T(128)}, f32[]{:T(128)}, f32[2,4,96,512]{3,2,1,0:T(8,128)S(1)}) fusion(f32[2,4,96,512]{3,2,1,0:T(8,128)S(1)} %fusion.47, f32[4,512]{1,0:T(4,128)S(1)} %fusion.65, f32[1536,256]{1,0:T(8,128)S(1)} %copy-done.4, f32[1536,256]{1,0:T(8,128)S(1)} %copy-done.2, f32[2,4,96,1536]{3,2,1,0:T(8,128)S(1)} %bitcast.69, ...), kind=kOutput, calls=%fused_computation.47 | convolution fusion | flops 7252869120 | bytes 13377544 | tf_op jit(solution)/shard_map/dot_general | solution.py:57
  408.8 38.4 %all-reduce = (f32[]{:T(128)}, f32[]{:T(128)}) all-reduce(f32[]{:T(128)} %get-tuple-element.3, f32[]{:T(128)} %get-tuple-element.2), channel_id=1, replica_groups=mesh['mem'=4,'lat'=2,'lon'=4] {'mem','lat','lon'}, use_global_device_ids=true, to_apply=%region_2.3 | all-reduce | flops 2 | bytes 16 | tf_op jit(solution)/shard_map/psum | solution.py:40
  448.3 1.0 multiply_reduce_fusion.3
  449.3 41.4 %psum.45 = f32[]{:T(128)} all-reduce(f32[]{:T(128)} %multiply_reduce_fusion.3), channel_id=1, replica_groups=mesh['mem'=4,'lat'=2,'lon'=4] {'mem','lat','lon'}, use_global_device_ids=true, to_apply=%region_9.10 | all-reduce | flops 1 | bytes 8 | tf_op jit(solution)/shard_map/psum | solution.py:40
  492.3 1.0 copy-done.9
  493.7 10.5 %multiply_reduce_fusion = f32[4,96,1536]{2,1,0:T(8,128)S(1)} fusion(f32[2,4,96,1536]{3,2,1,0:T(8,128)} %reshape.157, f32[256,1536]{1,0:T(8,128)S(1)} %copy-done.11, f32[256,1536]{1,0:T(8,128)S(1)} %copy-done.9, f32[2,4,96,512]{3,2,1,0:T(8,128)S(1)} %multiply_add_fusion.2, f32[4,512]{1,0:T(4,128)S(1)} %fusion.65), kind=kOutput, calls=%fused_computation.8 | convolution fusion | flops 7251492864 | bytes 11804672 | tf_op jit(solution)/shard_map/dot_general | solution.py:81
  504.7 55.9 %all_to_all.66 = f32[4,4,96,384]{3,2,1,0:T(8,128)S(1)} all-to-all(f32[4,4,96,384]{3,2,1,0:T(8,128)S(1)} %pad_maximum_fusion.1), channel_id=1, replica_groups=mesh['mem'=4,'lat'=2,'lon'=4] {'lon'}, dimensions={0} | all-to-all | bytes 4718592 | tf_op jit(solution)/shard_map/all_to_all | solution.py:91
  560.6 1.6 copy.45
  562.2 3.2 reshape.153
  565.5 54.8 %all-reduce.6.cloned.1.call-done = f32[589824]{0:T(1024)} async-done(((f32[589824]{0:T(1024)}), f32[589824]{0:T(1024)}) %all-reduce.6.cloned.1.call-update) | async-done | bytes 2359312 | tf_op jit(solution)/shard_map/psum | solution.py:36
  620.2 24.5 %gather_fusion.1 = f32[2048]{0:T(1024)S(1)} fusion(f32[589824]{0:T(1024)} %all-reduce.6.cloned.1.call-done, s32[2048]{0:T(1024)S(1)} %broadcast_clamp_fusion), kind=kCustom, calls=%fused_computation.1 | custom fusion | bytes 24576 | tf_op jit(solution)/shard_map/gather | solution.py:94
  644.7 12.8 %scatter_custom_fusion.2 = f32[589824]{0:T(1024)} fusion(s32[2048]{0:T(1024)S(1)} %bitcast.87, f32[2048]{0:T(1024)S(1)} %mul.240, f32[]{:T(128)} %constant.20.clone.1), kind=kCustom, calls=%fused_computation.73 | custom fusion | flops 2048 | bytes 2359300 | tf_op jit(solution)/shard_map/scatter-add | solution.py:53
  657.5 3.4 reshape.154
  661.0 3.2 copy.46
  664.2 58.4 %all_to_all.67 = f32[4,384,384]{2,0,1:T(4,128)S(1)} all-to-all(f32[4,384,384]{2,0,1:T(4,128)S(1)} %copy.46), channel_id=1, replica_groups=mesh['mem'=4,'lat'=2,'lon'=4] {'lon'}, dimensions={1} | all-to-all | bytes 4718592 | tf_op jit(solution)/shard_map/all_to_all | solution.py:70
  723.6 0.6 copy-done.3
  725.2 9.5 %multiply_reduce_fusion.2 = (f32[]{:T(128)}, f32[2,4,96,512]{3,2,1,0:T(8,128)}) fusion(f32[2,4,96,512]{3,2,1,0:T(8,128)S(1)} %copy-done.7, f32[4,512]{1,0:T(4,128)S(1)} %fusion.65, f32[1536,256]{1,0:T(8,128)S(1)} %copy-done.5, f32[1536,256]{1,0:T(8,128)S(1)} %copy-done.3, f32[2,4,96,1536]{3,2,1,0:T(8,128)S(1)} %bitcast.71, f32[4,96,1536]{2,1,0:T(8,128)S(1)} %bitcast.74), kind=kOutput, calls=%fused_computation.41 | convolution fusion | flops 7252082688 | bytes 13377540 | tf_op jit(solution)/shard_map/dot_general | solution.py:57
  734.7 38.3 %psum.47 = f32[]{:T(128)} all-reduce(f32[]{:T(128)} %get-tuple-element.17), channel_id=1, replica_groups=mesh['mem'=4,'lat'=2,'lon'=4] {'mem','lat','lon'}, use_global_device_ids=true, to_apply=%region_14.15 | all-reduce | flops 1 | bytes 8 | tf_op jit(solution)/shard_map/psum | solution.py:96
  774.2 4.3 multiply_subtract_fusion
  (58 shorter events, 6.1 us)
Async XLA Ops:
  29.4 60.3 %all-to-all-start.1 = ((f32[4,384,384]{2,0,1:T(4,128)}), f32[4,384,384]{2,0,1:T(4,128)}, u32[]{:S(2)}, u32[]{:S(2)}) async-start(f32[4,384,384]{2,0,1:T(4,128)} %copy.38), calls=%async_computation.1 | async-start | bytes 4718592 | tf_op jit(solution)/shard_map/all_to_all | solution.py:70
  40.6 53.8 %copy-start.13 = (s32[4]{0:T(128)S(1)}, s32[4]{0:T(128)}, u32[]{:S(2)}) copy-start(s32[4]{0:T(128)} %param.11) | copy-start | bytes 52
  89.6 57.9 %all-to-all-start = ((bf16[2,4,384,384]{3,1,0,2:T(4,128)(2,1)}), bf16[2,4,384,384]{3,1,0,2:T(4,128)(2,1)}, u32[]{:S(2)}, u32[]{:S(2)}) async-start(bf16[2,4,384,384]{3,1,0,2:T(4,128)(2,1)} %copy.36), calls=%async_computation | async-start | bytes 4718592 | tf_op jit(solution)/shard_map/all_to_all | solution.py:67
  94.1 201.3 %all-reduce.4.cloned.1.call-start = ((), (), s32[]{:S(2)}) async-start(), calls=%async_computation.6 | async-start | bytes 4718592 | tf_op jit(solution)/shard_map/psum | solution.py:36
  100.4 59.2 %copy-start.1 = (f32[1536,256]{1,0:T(8,128)}, f32[1536,256]{1,0:T(8,128)S(1)}, u32[]{:S(2)}) copy-start(f32[1536,256]{1,0:T(8,128)S(1)} %fusion.18) | copy-start | bytes 4718596
  159.6 10.9 %copy-start = (f32[2,4,96,1536]{3,2,1,0:T(8,128)S(1)}, f32[2,4,96,1536]{3,2,1,0:T(8,128)}, u32[]{:S(2)}) copy-start(f32[2,4,96,1536]{3,2,1,0:T(8,128)} %reshape.157) | copy-start | bytes 14155780
  159.6 10.9 %copy-start.8 = (f32[256,1536]{1,0:T(8,128)S(1)}, f32[256,1536]{1,0:T(8,128)}, u32[]{:S(2)}) copy-start(f32[256,1536]{1,0:T(8,128)} %fusion.24) | copy-start | bytes 4718596
  159.6 11.0 %copy-start.10 = (f32[256,1536]{1,0:T(8,128)S(1)}, f32[256,1536]{1,0:T(8,128)}, u32[]{:S(2)}) copy-start(f32[256,1536]{1,0:T(8,128)} %fusion.27) | copy-start | bytes 4718596
  240.6 379.7 %all-reduce.6.cloned.1.call-start = ((), (), s32[]{:S(2)}) async-start(), calls=%async_computation.7 | async-start | bytes 4718592 | tf_op jit(solution)/shard_map/psum | solution.py:36
  240.6 79.3 %copy-start.12 = (f32[1,2048]{1,0:T(1,128)S(1)}, f32[1,2048]{1,0:T(1,128)}, u32[]{:S(2)}) copy-start(f32[1,2048]{1,0:T(1,128)} %param.8) | copy-start | bytes 24580
  339.4 59.2 %slice-start = ((s8[4718592]{0:T(1024)(128)(4,1)}), s8[4194304]{0:T(1024)(128)(4,1)S(1)}, s32[]{:S(2)}) async-start(s8[4718592]{0:T(1024)(128)(4,1)} %bitcast.68), calls=%async_computation.8 | async-start | bytes 8388608
  398.1 1.0 slice-start.1
  398.2 1.4 copy-start.2
  398.3 1.9 copy-start.4
  491.9 1.4 copy-start.9
  491.9 1.9 copy-start.11
  493.7 10.5 %copy-start.6 = (f32[2,4,96,512]{3,2,1,0:T(8,128)}, f32[2,4,96,512]{3,2,1,0:T(8,128)S(1)}, u32[]{:S(2)}) copy-start(f32[2,4,96,512]{3,2,1,0:T(8,128)S(1)} %multiply_add_fusion.2) | copy-start | bytes 4718596
  664.1 59.0 %slice-start.2 = ((s8[4718592]{0:T(1024)(128)(4,1)}), s8[4194304]{0:T(1024)(128)(4,1)S(1)}, s32[]{:S(2)}) async-start(s8[4718592]{0:T(1024)(128)(4,1)} %bitcast.70), calls=%async_computation.10 | async-start | bytes 8388608
  722.6 1.0 slice-start.3
  722.8 1.4 copy-start.3
  722.8 1.9 copy-start.5
  722.8 2.4 copy-start.7
Sparse Core Ops, SparseCore 0:
  240.7 54.7 all-reduce.3
  565.6 54.5 all-reduce.5
